TPU v7x, 32 devices: a whole 2x2x4 slice. The times are simulated.
32 devices in a mesh: seq: 8 (over y, x, core), head: 4 (over z).
Axes of the slice: x: 2, y: 2, z: 4, core: 2. Of those that a mesh axis runs over, the one named last changes fastest.
Arguments:
- query: bfloat16 [1024, 96, 128], P(('seq', 'head')), may hold values from -15.6 to 15.6
- key_new: bfloat16 [1024, 8, 128], P('seq', 'head'), may hold values from -6 to 6
- value_new: bfloat16 [1024, 8, 128], P('seq', 'head'), may hold values from -6 to 6
- key_old: bfloat16 [1024, 8, 128], P('seq', 'head'), may hold values from -6 to 6
- value_old: bfloat16 [1024, 8, 128], P('seq', 'head'), may hold values from -6 to 6
- offset: int32 [1], replicated, may hold values from 0 to 1023
- windows: int32 [8], P('head'), may hold values from 512 to 1024, as said below
- grad_out: bfloat16 [1024, 96, 128], P(('seq', 'head')), may hold values from -6 to 6
Outputs:
- grad_query: float32 [1024, 96, 128], P(('seq', 'head'))
- grad_key_new: float32 [1024, 8, 128], P('seq', 'head')
- grad_value_new: float32 [1024, 8, 128], P('seq', 'head')
- grad_key_old: float32 [1024, 8, 128], P('seq', 'head')
- grad_value_old: float32 [1024, 8, 128], P('seq', 'head')
Inputs may be any that keep to these rules, and one draw needn't show every extreme that they name: `windows`: one key-value head has a window of exactly 1024 tokens and another of exactly 512.
All inputs are finite; a program needn't handle non-finite values.
Results may differ from a plain program's by a relative error of at most 0.003.
Values may be sent and summed in bfloat16 or wider, within the bound.
A program may use at most 128 MiB of HBM per device.

v0:
```python
import math

import jax
import jax.numpy as jnp
from jax import lax
from jax.sharding import PartitionSpec as P


def score_tile(operand, partner):
    return jnp.einsum("qgjd,kgd->qgjk", operand, partner, preferred_element_type=jnp.float32)


def visible_mask(key_pos, query_pos, reaches):
    key_row = key_pos[None, None, None, :]
    query_col = query_pos[:, None, None, None]
    return (key_row <= query_col) & (key_row > query_col - reaches[None, :, None, None])


def shards(query, key_new, value_new, key_old, value_old, offset, windows, grad_out):
    queries, out_grads = (
        lax.all_to_all(query, "head", split_axis=1, concat_axis=0, tiled=True),
        lax.all_to_all(grad_out, "head", split_axis=1, concat_axis=0, tiled=True),
    )
    tok_rows, head_count, head_width = queries.shape
    group_count = key_new.shape[1]
    per_group = head_count // group_count
    seq_count = lax.axis_size("seq")
    seq_rank = lax.axis_index("seq")
    total_rows = tok_rows * seq_count
    score_scale = 1.0 / math.sqrt(head_width)
    queries = queries.reshape(tok_rows, group_count, per_group, head_width)
    out_grads = out_grads.reshape(tok_rows, group_count, per_group, head_width)
    first_query = seq_rank * tok_rows
    last_query = first_query + tok_rows - 1
    row_iota = jnp.arange(tok_rows, dtype=jnp.int32)
    query_pos = first_query + row_iota
    widest = jnp.max(windows)
    shift_at = offset[0]
    stored_pair = jnp.stack([key_old, value_old])
    new_home = jnp.stack([key_new, value_new])
    home_kv = jnp.concatenate([new_home, stored_pair])

    def old_positions(row_start, length):
        slot_index = row_start + jnp.arange(length, dtype=jnp.int32)
        return (slot_index - shift_at) % total_rows - total_rows

    def guarded(update, held_state, tile_pair, key_pos, allowed=True):
        touched = jnp.logical_and(
            allowed, jnp.any((key_pos <= last_query) & (key_pos > first_query - widest))
        )
        return lax.cond(
            touched,
            lambda state_in: update(state_in, tile_pair, key_pos),
            lambda state_in: state_in,
            held_state,
        )

    def stats_tile(held_state, tile_pair, key_pos):
        row_top, row_total, row_weighted = held_state
        seen = visible_mask(key_pos, query_pos, windows)
        masked = jnp.where(seen, score_scale * score_tile(queries, tile_pair[0]), -jnp.inf)
        weight_grad = score_tile(out_grads, tile_pair[1])
        new_top = jnp.maximum(row_top, jnp.max(masked, axis=-1))
        anchor = jnp.where(new_top == -jnp.inf, 0.0, new_top)
        shifted_exp = jnp.exp(masked - anchor[..., None])
        factor = jnp.exp(row_top - anchor)
        return (
            new_top,
            row_total * factor + jnp.sum(shifted_exp, axis=-1),
            row_weighted * factor + jnp.sum(shifted_exp * weight_grad, axis=-1),
        )

    stat_shape = (tok_rows, group_count, per_group)
    empty_stats = (
        jnp.full(stat_shape, -jnp.inf, jnp.float32),
        jnp.zeros(stat_shape, jnp.float32),
        jnp.zeros(stat_shape, jnp.float32),
    )
    key_block = tok_rows * math.gcd(seq_count, 4)
    block_total = total_rows // key_block
    everything = lax.all_gather(home_kv, "seq", axis=1, tiled=True)

    def collect_stats(block_index, running):
        row_start = block_index * key_block
        key_piece = lax.dynamic_slice_in_dim(everything, row_start, key_block, 1)
        running = guarded(
            stats_tile, running, key_piece[0:2], row_start + jnp.arange(key_block, dtype=jnp.int32)
        )
        return guarded(stats_tile, running, key_piece[2:4], old_positions(row_start, key_block))

    running = lax.fori_loop(0, block_total, collect_stats, empty_stats)
    log_total = running[0] + jnp.log(running[1])
    row_delta = running[2] / running[1]

    def grad_tile(held_state, tile_pair, key_pos):
        query_grad, held_sums = held_state
        seen = visible_mask(key_pos, query_pos, windows)
        weights = jnp.where(
            seen,
            jnp.exp(score_scale * score_tile(queries, tile_pair[0]) - log_total[..., None]),
            0.0,
        )
        weight_grad = score_tile(out_grads, tile_pair[1])
        dscore = (weights * (weight_grad - row_delta[..., None])).astype(jnp.bfloat16)
        weights_low = weights.astype(jnp.bfloat16)
        query_grad = query_grad + score_scale * jnp.einsum(
            "qgjk,kgd->qgjd", dscore, tile_pair[0], preferred_element_type=jnp.float32
        )
        key_part = score_scale * jnp.einsum(
            "qgjk,qgjd->kgd", dscore, queries, preferred_element_type=jnp.float32
        )
        value_part = jnp.einsum(
            "qgjk,qgjd->kgd", weights_low, out_grads, preferred_element_type=jnp.float32
        )
        return (query_grad, held_sums + jnp.stack([key_part, value_part]))

    zero_query = jnp.zeros(queries.shape, jnp.float32)
    zero_terms = jnp.zeros((4, total_rows, group_count, head_width), jnp.float32)

    def collect_grads(block_index, held_state):
        query_grad, grad_terms = held_state
        row_start = block_index * key_block
        key_piece = lax.dynamic_slice_in_dim(everything, row_start, key_block, 1)
        term_piece = lax.dynamic_slice_in_dim(grad_terms, row_start, key_block, 1)
        query_grad, low_terms = guarded(
            grad_tile,
            (query_grad, term_piece[0:2]),
            key_piece[0:2],
            row_start + jnp.arange(key_block, dtype=jnp.int32),
        )
        query_grad, high_terms = guarded(
            grad_tile,
            (query_grad, term_piece[2:4]),
            key_piece[2:4],
            old_positions(row_start, key_block),
        )
        grad_terms = lax.dynamic_update_slice_in_dim(
            grad_terms, jnp.concatenate([low_terms, high_terms]), row_start, 1
        )
        return (query_grad, grad_terms)

    query_grad, grad_terms = lax.fori_loop(0, block_total, collect_grads, (zero_query, zero_terms))
    moving_grads = lax.psum_scatter(grad_terms, "seq", scatter_dimension=1, tiled=True)
    old_grads = moving_grads[2:4]
    grad_query = lax.all_to_all(
        query_grad.reshape(tok_rows, head_count, head_width),
        "head",
        split_axis=0,
        concat_axis=1,
        tiled=True,
    )
    return (grad_query, moving_grads[0], moving_grads[1], old_grads[0], old_grads[1])


def solution(mesh):
    placed = (
        P(("seq", "head"), None, None),
        P("seq", "head", None),
        P("seq", "head", None),
        P("seq", "head", None),
        P("seq", "head", None),
        P(),
        P("head"),
        P(("seq", "head"), None, None),
    )
    return jax.shard_map(
        shards,
        mesh=mesh,
        in_specs=placed,
        out_specs=(
            P(("seq", "head"), None, None),
            P("seq", "head", None),
            P("seq", "head", None),
            P("seq", "head", None),
            P("seq", "head", None),
        ),
        check_vma=False,
    )
```

profile of v0, /device:TPU:1, one launch (start us, length us, event | category | flops | bytes accessed | tf_op | source)
XLA Modules:
  0.0 262.4 jit_solution(17107480988480357261)
XLA Ops:
  7.2 0.9 copy_bitcast_fusion.2
  8.1 0.9 copy_bitcast_fusion
  9.8 2.3 copy.49
  12.1 5.4 %all-to-all-start = ((bf16[32,96,128]{2,0,1:T(8,128)(2,1)}), bf16[32,96,128]{2,0,1:T(8,128)(2,1)S(1)}, u32[]{:S(2)}, u32[]{:S(2)}) async-start(bf16[32,96,128]{2,0,1:T(8,128)(2,1)} %copy.49), calls=%async_computation | async-start | bytes 1572864 | tf_op jit(solution)/shard_map/all_to_all | solution.py:21
  17.5 2.3 copy.51
  19.8 17.3 %all-to-all-done = bf16[32,96,128]{2,0,1:T(8,128)(2,1)S(1)} async-done(((bf16[32,96,128]{2,0,1:T(8,128)(2,1)}), bf16[32,96,128]{2,0,1:T(8,128)(2,1)S(1)}, u32[]{:S(2)}, u32[]{:S(2)}) %all-to-all-start) | async-done | bytes 786464 | tf_op jit(solution)/shard_map/all_to_all | solution.py:21
  37.2 3.5 %all-to-all-start.1 = ((bf16[32,96,128]{2,0,1:T(8,128)(2,1)}), bf16[32,96,128]{2,0,1:T(8,128)(2,1)S(1)}, u32[]{:S(2)}, u32[]{:S(2)}) async-start(bf16[32,96,128]{2,0,1:T(8,128)(2,1)} %copy.51), calls=%async_computation.1 | async-start | bytes 1572864 | tf_op jit(solution)/shard_map/all_to_all | solution.py:22
  42.1 18.2 %all-to-all-done.1 = bf16[32,96,128]{2,0,1:T(8,128)(2,1)S(1)} async-done(((bf16[32,96,128]{2,0,1:T(8,128)(2,1)}), bf16[32,96,128]{2,0,1:T(8,128)(2,1)S(1)}, u32[]{:S(2)}, u32[]{:S(2)}) %all-to-all-start.1) | async-done | bytes 786464 | tf_op jit(solution)/shard_map/all_to_all | solution.py:22
  60.3 1.0 copy.52
  61.3 30.2 %while.38 = (s32[]{:T(128)}, f32[128,2,12]{0,2,1:T(8,128)S(1)}, f32[128,2,12]{0,2,1:T(8,128)S(1)}, f32[128,2,12]{0,2,1:T(8,128)S(1)}, s32[]{:T(128)}, /*index=5*...) while((s32[]{:T(128)}, f32[128,2,12]{0,2,1:T(8,128)S(1)}, ...), condition=%wide.region_14.15_spmd.clone, body=%wide.region_1.14_spmd.clone.sunk | while | flops 1649078912 | bytes 61570112 | solution.py:91
  61.3 1.4 fusion.97
  64.7 1.1 constant_dynamic-slice_fusion.13
  65.8 4.6 %conditional.12 = ((f32[128,2,12]{0,2,1:T(8,128)S(1)}, f32[128,2,12]{0,2,1:T(8,128)S(1)}, f32[128,2,12]{0,2,1:T(8,128)S(1)})) conditional(s32[]{:T(128)} %convert_element_type.71, (f32[128,2,12]{0,2,1:T(8,128)S(1)}, f32[128,2,12]{0,2,1:T(8,128)S(1)}, f32[128,2,12]{0,2,1:T(8,128)S(1)}) %tuple.141, (s32[512]{0:T(512)S(1)}, s32[128]{0:T(128)S(1)}, ...), branch_computations={%region_4.4_spmd, %region_5.8_spmd} | conditional | flops 824530176 | bytes 25017412 | solution.py:51
  66.2 1.0 fusion.6
  67.3 1.8 fusion.4
  69.1 1.3 fusion.5
  70.4 1.1 constant_dynamic-slice_fusion.14
  71.5 6.4 %conditional.13 = ((f32[128,2,12]{0,2,1:T(8,128)S(1)}, f32[128,2,12]{0,2,1:T(8,128)S(1)}, f32[128,2,12]{0,2,1:T(8,128)S(1)})) conditional(s32[]{:T(128)} %convert_element_type.70, (f32[128,2,12]{0,2,1:T(8,128)S(1)}, f32[128,2,12]{0,2,1:T(8,128)S(1)}, f32[128,2,12]{0,2,1:T(8,128)S(1)}) %get-tuple-element.1282, (s32[512]{0:T(512)S(1)}, ...), branch_computations={%region_9.9_spmd, %region_10.13_spmd} | conditional | flops 824530176 | bytes 25013316 | solution.py:51
  71.9 1.9 fusion.14
  73.9 2.8 %fusion.12 = f32[128,2,12]{0,2,1:T(8,128)S(1)} fusion(f32[2,512,128,12]{2,1,3,0:T(8,128)S(1)} %get-tuple-element.947, f32[128,2,12]{0,2,1:T(8,128)S(1)} %get-tuple-element.938, pred[128,2,512]{0,2,1:T(8,128)(4,1)S(1)} %compare_and_fusion.1, bf16[128,2,12,128]{3,0,2,1:T(8,128)(2,1)S(1)} %copy-done.8, bf16[4,512,2,128]{3,1,2,0:T(8,128)(2,1)} %get-tuple-element.743), kind=kOutput, calls=%fused_computation.21 | convolution fusion | flops 410514432 | bytes 7495680 | tf_op jit(solution)/shard_map/while/body/eval_jaxpr/cond/branch_1_fun/qgjd,kgd->qgjk/dot_general | solution.py:10
  76.6 1.3 fusion.13
  78.0 1.4 fusion.97
  81.4 1.1 constant_dynamic-slice_fusion.13
  82.5 1.6 copy-done.6
  84.0 1.0 constant_dynamic-slice_fusion.14
  85.1 6.4 %conditional.13 = ((f32[128,2,12]{0,2,1:T(8,128)S(1)}, f32[128,2,12]{0,2,1:T(8,128)S(1)}, f32[128,2,12]{0,2,1:T(8,128)S(1)})) conditional(s32[]{:T(128)} %convert_element_type.70, (f32[128,2,12]{0,2,1:T(8,128)S(1)}, f32[128,2,12]{0,2,1:T(8,128)S(1)}, f32[128,2,12]{0,2,1:T(8,128)S(1)}) %get-tuple-element.1282, (s32[512]{0:T(512)S(1)}, ...), branch_computations={%region_9.9_spmd, %region_10.13_spmd} | conditional | flops 824530176 | bytes 25013316 | solution.py:51
  85.5 1.9 fusion.14
  87.4 2.8 %fusion.12 = f32[128,2,12]{0,2,1:T(8,128)S(1)} fusion(f32[2,512,128,12]{2,1,3,0:T(8,128)S(1)} %get-tuple-element.947, f32[128,2,12]{0,2,1:T(8,128)S(1)} %get-tuple-element.938, pred[128,2,512]{0,2,1:T(8,128)(4,1)S(1)} %compare_and_fusion.1, bf16[128,2,12,128]{3,0,2,1:T(8,128)(2,1)S(1)} %copy-done.8, bf16[4,512,2,128]{3,1,2,0:T(8,128)(2,1)} %get-tuple-element.743), kind=kOutput, calls=%fused_computation.21 | convolution fusion | flops 410514432 | bytes 7495680 | tf_op jit(solution)/shard_map/while/body/eval_jaxpr/cond/branch_1_fun/qgjd,kgd->qgjk/dot_general | solution.py:10
  90.2 1.3 fusion.13
  91.6 1.3 broadcast_in_dim.67
  92.9 2.5 broadcast_in_dim.68.clone
  95.4 50.0 %while.39 = (s32[]{:T(128)}, f32[128,2,12,128]{3,0,2,1:T(8,128)}, f32[4,1024,2,128]{3,0,2,1:T(4,128)}, s32[]{:T(128)}, s32[]{:T(128)}, /*index=5*/s32[]{:T(128)}...) while((s32[]{:T(128)}, f32[128,2,12,128]{3,0,2,1:T(8,128)}, ...), condition=%wide.region_22.23_spmd.clone, body=%wide.region_15.22_spmd.clone.sunk | while | flops 4062071296 | bytes 139046144 | solution.py:142
  95.4 1.3 fusion.99
  98.5 2.3 constant_dynamic-slice_fusion.16
  100.8 3.1 %constant_dynamic-slice_fusion.15 = (f32[2,512,2,128]{3,0,2,1:T(2,128)S(1)}, f32[2,512,2,128]{3,0,2,1:T(2,128)S(1)}) fusion(f32[4,1024,2,128]{3,0,2,1:T(4,128)} %get-tuple-element.1248, s32[]{:T(128)S(6)} %add.319, s32[]{:T(128)S(6)} %select_n.140), kind=kLoop, calls=%fused_computation.121.clone.1 | loop fusion | bytes 4194312 | tf_op jit(solution)/shard_map/while/body/eval_jaxpr/slice | solution.py:133
  104.0 9.6 %conditional.14 = ((f32[128,2,12,128]{3,0,2,1:T(8,128)}, f32[2,512,2,128]{3,1,2,0:T(8,128)S(1)})) conditional(s32[]{:T(128)} %convert_element_type.73, (f32[128,2,12,128]{3,0,2,1:T(8,128)}, f32[2,512,2,128]{3,1,2,0:T(8,128)S(1)}) %tuple.148, (s32[512]{0:T(512)S(1)}, s32[128]{0:T(128)S(1)}, s32[2]{0:T(128)S(1)}, ...), branch_computations={%region_18.18_spmd, %region_19.19_spmd} | conditional | flops 2030764288 | bytes 60083344 | solution.py:51
  104.4 1.9 fusion.35
  106.4 1.1 fusion.30
  107.6 2.0 fusion.21
  109.6 1.0 fusion.29
  110.6 1.8 bitcast_add_fusion
  112.7 0.9 copy-done.1
  113.6 8.7 %conditional.15 = ((f32[128,2,12,128]{3,0,2,1:T(8,128)}, f32[2,512,2,128]{3,1,2,0:T(8,128)S(1)})) conditional(s32[]{:T(128)} %convert_element_type.72, (f32[128,2,12,128]{3,0,2,1:T(8,128)}, f32[2,512,2,128]{3,1,2,0:T(8,128)S(1)}) %tuple.150, (s32[512]{0:T(512)S(1)}, s32[128]{0:T(128)S(1)}, s32[2]{0:T(128)S(1)}, ...), branch_computations={%region_20.20_spmd, %region_21.21_spmd} | conditional | flops 2030764288 | bytes 60083344 | solution.py:51
  114.0 1.9 fusion.57
  116.0 1.1 fusion.52
  117.2 2.0 fusion.43
  119.2 1.8 bitcast_add_fusion.1
  121.1 1.0 fusion.51
  122.5 2.7 %copy_dynamic-update-slice_fusion.2 = f32[4,1024,2,128]{3,0,2,1:T(4,128)} fusion(f32[4,1024,2,128]{3,0,2,1:T(4,128)} %get-tuple-element.1248, s32[]{:T(128)S(6)} %select_n.140, f32[4,512,2,128]{3,1,2,0:T(8,128)S(1)} %pad_maximum_fusion.3), kind=kLoop, calls=%fused_computation.107.clone.1 | loop fusion | bytes 4194308 | tf_op jit(solution)/shard_map/while/body/eval_jaxpr/dynamic_update_slice | solution.py:137
  125.2 1.3 fusion.99
  128.3 2.3 constant_dynamic-slice_fusion.16
  130.5 3.1 %constant_dynamic-slice_fusion.15 = (f32[2,512,2,128]{3,0,2,1:T(2,128)S(1)}, f32[2,512,2,128]{3,0,2,1:T(2,128)S(1)}) fusion(f32[4,1024,2,128]{3,0,2,1:T(4,128)} %get-tuple-element.1248, s32[]{:T(128)S(6)} %add.319, s32[]{:T(128)S(6)} %select_n.140), kind=kLoop, calls=%fused_computation.121.clone.1 | loop fusion | bytes 4194312 | tf_op jit(solution)/shard_map/while/body/eval_jaxpr/slice | solution.py:133
  133.8 8.7 %conditional.15 = ((f32[128,2,12,128]{3,0,2,1:T(8,128)}, f32[2,512,2,128]{3,1,2,0:T(8,128)S(1)})) conditional(s32[]{:T(128)} %convert_element_type.72, (f32[128,2,12,128]{3,0,2,1:T(8,128)}, f32[2,512,2,128]{3,1,2,0:T(8,128)S(1)}) %tuple.150, (s32[512]{0:T(512)S(1)}, s32[128]{0:T(128)S(1)}, s32[2]{0:T(128)S(1)}, ...), branch_computations={%region_20.20_spmd, %region_21.21_spmd} | conditional | flops 2030764288 | bytes 60083344 | solution.py:51
  134.2 1.9 fusion.57
  136.2 1.1 fusion.52
  137.4 2.0 fusion.43
  139.5 1.8 bitcast_add_fusion.1
  141.3 1.0 fusion.51
  142.7 2.7 %copy_dynamic-update-slice_fusion.2 = f32[4,1024,2,128]{3,0,2,1:T(4,128)} fusion(f32[4,1024,2,128]{3,0,2,1:T(4,128)} %get-tuple-element.1248, s32[]{:T(128)S(6)} %select_n.140, f32[4,512,2,128]{3,1,2,0:T(8,128)S(1)} %pad_maximum_fusion.3), kind=kLoop, calls=%fused_computation.107.clone.1 | loop fusion | bytes 4194308 | tf_op jit(solution)/shard_map/while/body/eval_jaxpr/dynamic_update_slice | solution.py:137
  145.4 3.5 %copy.53 = f32[128,24,128]{2,1,0:T(8,128)} copy(f32[128,24,128]{2,0,1:T(8,128)} %bitcast.202) | data formatting | bytes 3145728 | tf_op jit(solution)/shard_map/reshape | solution.py:146
  149.0 3.6 %all-to-all-start.2 = ((f32[128,24,128]{2,1,0:T(8,128)}), f32[128,24,128]{2,1,0:T(8,128)S(1)}, u32[]{:S(2)}, u32[]{:S(2)}) async-start(f32[128,24,128]{2,1,0:T(8,128)} %copy.53), calls=%async_computation.2 | async-start | bytes 3145728 | tf_op jit(solution)/shard_map/all_to_all | solution.py:145
  154.6 96.5 %all-reduce.3.cloned.1.call-done = f32[4,1024,2,128]{3,0,2,1:T(4,128)} async-done(((f32[4,1024,2,128]{3,0,2,1:T(4,128)}), f32[4,1024,2,128]{3,0,2,1:T(4,128)}) %all-reduce.3.cloned.1.call-update) | async-done | bytes 4194320
  251.1 3.1 %constant_dynamic-slice_fusion.8 = (f32[1,128,2,128]{3,0,2,1:T(1,128)}, f32[1,128,2,128]{3,0,2,1:T(1,128)}, f32[1,128,2,128]{3,0,2,1:T(1,128)}, f32[1,128,2,128]{3,0,2,1:T(1,128)}) fusion(f32[4,1024,2,128]{3,0,2,1:T(4,128)} %all-reduce.3.cloned.1.call-done, u32[]{:T(128)S(6)} %convert.2, u32[]{:T(128)S(6)} %multiply.9, u32[]{:T(128)S(6)} %convert.1, ...), kind=kLoop, calls=%fused_computation.132 | loop fusion | bytes 1048592 | tf_op jit(solution)/shard_map/slice | solution.py:152
  254.2 1.3 copy.54
  (96 shorter events, 9.3 us)
Async XLA Ops:
  7.2 33.5 %copy-start.11 = (s32[2]{0:T(128)S(1)}, s32[2]{0:T(128)}, u32[]{:S(2)}) copy-start(s32[2]{0:T(128)} %param.26) | copy-start | bytes 28
  7.2 54.1 %all-gather.2.cloned.1.call-start = ((), (), s32[]{:S(2)}) async-start(), calls=%async_computation.3 | async-start | bytes 2359296 | tf_op jit(solution)/shard_map/all_gather | solution.py:81
  12.1 25.1 %all-to-all-start = ((bf16[32,96,128]{2,0,1:T(8,128)(2,1)}), bf16[32,96,128]{2,0,1:T(8,128)(2,1)S(1)}, u32[]{:S(2)}, u32[]{:S(2)}) async-start(bf16[32,96,128]{2,0,1:T(8,128)(2,1)} %copy.49), calls=%async_computation | async-start | bytes 1572864 | tf_op jit(solution)/shard_map/all_to_all | solution.py:21
  37.2 23.1 %all-to-all-start.1 = ((bf16[32,96,128]{2,0,1:T(8,128)(2,1)}), bf16[32,96,128]{2,0,1:T(8,128)(2,1)S(1)}, u32[]{:S(2)}, u32[]{:S(2)}) async-start(bf16[32,96,128]{2,0,1:T(8,128)(2,1)} %copy.51), calls=%async_computation.1 | async-start | bytes 1572864 | tf_op jit(solution)/shard_map/all_to_all | solution.py:22
  65.8 4.6 %copy-start.6 = (bf16[4,1024,2,128]{3,1,2,0:T(8,128)(2,1)S(1)}, bf16[4,1024,2,128]{3,1,2,0:T(8,128)(2,1)}, u32[]{:S(2)}) copy-start(bf16[4,1024,2,128]{3,1,2,0:T(8,128)(2,1)} %get-tuple-element.1219) | copy-start | bytes 6291460 | tf_op jit(solution)/shard_map/while
  65.8 1.4 copy-start.7
  71.5 2.3 copy-start.8
  82.5 1.6 copy-start.6
  85.1 2.3 copy-start.8
  104.1 2.3 copy-start.9
  106.4 1.2 copy-start.4
  107.6 3.0 %copy-start = (f32[128,2,12,128]{3,0,2,1:T(8,128)S(1)}, f32[128,2,12,128]{3,0,2,1:T(8,128)}, u32[]{:S(2)}) copy-start(f32[128,2,12,128]{3,0,2,1:T(8,128)} %get-tuple-element.767) | copy-start | bytes 4718596 | tf_op jit(solution)/shard_map/while/body/eval_jaxpr/cond
  112.5 1.1 copy-start.1
  113.6 2.3 copy-start.10
  115.9 1.2 copy-start.5
  117.2 2.0 copy-start.2
  121.1 1.3 copy-start.3
  133.9 2.3 copy-start.10
  136.2 1.2 copy-start.5
  137.4 2.0 copy-start.2
  141.3 1.3 copy-start.3
  145.4 7.9 %copy-start.12 = (u32[32]{0:T(128)S(1)}, u32[32]{0:T(128)}, u32[]{:S(2)}) copy-start(u32[32]{0:T(128)} %constant.188) | copy-start | bytes 388
  149.0 105.2 %all-to-all-start.2 = ((f32[128,24,128]{2,1,0:T(8,128)}), f32[128,24,128]{2,1,0:T(8,128)S(1)}, u32[]{:S(2)}, u32[]{:S(2)}) async-start(f32[128,24,128]{2,1,0:T(8,128)} %copy.53), calls=%async_computation.2 | async-start | bytes 3145728 | tf_op jit(solution)/shard_map/all_to_all | solution.py:145
  152.5 98.6 %all-reduce.3.cloned.1.call-start = ((), (), s32[]{:S(2)}) async-start(), calls=%async_computation.4 | async-start | bytes 8388608
Sparse Core Ops, SparseCore 0:
  9.9 30.2 all-gather.1
  156.6 94.4 all-reduce.2
where the time goes:
time: 264 us; the launch traced here: 262 us
  waiting for transfers between devices  133 us (50%)
  local copies, waits for them, and re-layouts  43.4 us (16%)
  matrix products  36 us (14%)
  other arithmetic  16.5 us (6%)
  between operations  15.4 us (6%)
  starting transfers between devices  12.5 us (5%)
  loops' own time  5.76 us (2%)
    unnamed x3, waiting for transfers between devices  97.3 us
    dot_general x12, matrix products, score_tile(): jnp.einsum('qgjd,kgd->qgjk', operand, partner, preferred_element_type=jnp...  24.1 us
    all_to_all x1, waiting for transfers between devices, shards(): lax.all_to_all(grad_out, 'head', split_axis=1, concat_axis=0, tiled=True)  18.2 us
    all_to_all x1, waiting for transfers between devices, shards(): lax.all_to_all(query, 'head', split_axis=1, concat_axis=0, tiled=True)  17.3 us
    slice x2, local copies, waits for them, and re-layouts, collect_grads(): term_piece[2:4]  6.24 us
    dot_general x3, matrix products, grad_tile(): jnp.einsum('qgjk,kgd->qgjd', dscore, tile_pair[0], preferred_element_type...  5.51 us
    dynamic_update_slice x2, local copies, waits for them, and re-layouts, collect_grads(): lax.dynamic_update_slice_in_dim(grad_terms, jnp.concatenate([low_terms, h...  5.41 us
    all_to_all x1, starting transfers between devices, shards(): lax.all_to_all(query, 'head', split_axis=1, concat_axis=0, tiled=True)  5.41 us
  transfers between devices with their start and end apart: 5, of which 3 were waited for; matrix products, arithmetic and copies ran while one was open for 4% of the time, Pallas kernels for 0%

commit v1 on v0

v1 whole, which is shorter than its diff:
```python
import functools
import math

import jax
import jax.numpy as jnp
from jax import lax
from jax.experimental import pallas as pl
from jax.experimental.pallas import tpu as pltpu
from jax.sharding import PartitionSpec as P

NT = (((1,), (1,)), ((), ()))
NN = (((1,), (0,)), ((), ()))


def dot(a, b, dims):
    return lax.dot_general(a, b, dims, preferred_element_type=jnp.float32)


def band_kernel(
    heads, reach, win_ref, q_ref, do_ref, k_ref, kt_ref, v_ref, dq_ref, dk_ref, dv_ref, bias, dk_sum, dv_sum
):
    group, step = pl.program_id(0), pl.program_id(1)
    blocks, _, rows, width = q_ref.shape
    tokens = blocks * rows
    span = k_ref.shape[1]
    scale = 1.0 / math.sqrt(width)

    @pl.when(step == 0)
    def _():
        window = win_ref[group]
        place = lax.broadcasted_iota(jnp.int32, (span, tokens), 0) - reach
        token = lax.broadcasted_iota(jnp.int32, (span, tokens), 1)
        seen = (place <= token) & (place > token - window)
        bias[...] = jnp.where(seen, 0.0, -jnp.inf)

    q = jnp.concatenate([q_ref[:, h].reshape(tokens, width) for h in range(heads)], 0)
    do = jnp.concatenate([do_ref[:, h].reshape(tokens, width) for h in range(heads)], 0)
    keys, values = k_ref[0], v_ref[0]
    scores = dot(keys, q, NT) + jnp.concatenate([bias[...]] * heads, 1)
    top = jnp.max(scores, axis=0, keepdims=True)
    grown = jnp.exp2((scores - top) * (scale * math.log2(math.e)))
    total = jnp.sum(grown, axis=0, keepdims=True)
    weight_grad = dot(values, do, NT)
    inverse = 1.0 / total
    delta = jnp.sum(grown * weight_grad, axis=0, keepdims=True) * inverse
    weights = grown * inverse
    dscore = (weights * (weight_grad - delta)).astype(jnp.bfloat16)
    dk_part = dot(dscore, q, NN)
    dv_part = dot(weights.astype(jnp.bfloat16), do, NN)
    dqt = dot(kt_ref[0], dscore, NN) * scale
    for h in range(heads):
        piece = dqt[:, h * tokens : (h + 1) * tokens].T
        dq_ref[:, h] = piece.reshape(blocks, rows, width).astype(dq_ref.dtype)

    @pl.when(step == 0)
    def _():
        dk_sum[...] = dk_part
        dv_sum[...] = dv_part

    @pl.when(step > 0)
    def _():
        dk_sum[...] += dk_part
        dv_sum[...] += dv_part

    @pl.when(step == pl.num_programs(1) - 1)
    def _():
        dk_ref[0] = (dk_sum[...] * scale).astype(dk_ref.dtype)
        dv_ref[0] = dv_sum[...].astype(dv_ref.dtype)


def band(windows, q, do, k, kt, v, reach):
    blocks, all_heads, rows, width = q.shape
    groups, span, _ = k.shape
    tokens = blocks * rows
    per_group = all_heads // groups
    heads = max(
        h for h in (1, 2, 4) if per_group % h == 0 and (h <= 1 or h * tokens * span <= 700_000)
    )
    steps = per_group // heads
    row_spec = pl.BlockSpec((blocks, heads, rows, width), lambda g, s: (0, g * steps + s, 0, 0))
    key_spec = pl.BlockSpec((1, span, width), lambda g, s: (g, 0, 0))
    return pl.pallas_call(
        functools.partial(band_kernel, heads, reach),
        grid=(groups, steps),
        in_specs=[
            pl.BlockSpec(memory_space=pltpu.SMEM),
            row_spec,
            row_spec,
            key_spec,
            pl.BlockSpec((1, width, span), lambda g, s: (g, 0, 0)),
            key_spec,
        ],
        out_specs=[row_spec, key_spec, key_spec],
        out_shape=[
            jax.ShapeDtypeStruct(q.shape, jnp.bfloat16),
            jax.ShapeDtypeStruct(k.shape, jnp.bfloat16),
            jax.ShapeDtypeStruct(k.shape, jnp.bfloat16),
        ],
        scratch_shapes=[
            pltpu.VMEM((span, tokens), jnp.float32),
            pltpu.VMEM((span, width), jnp.float32),
            pltpu.VMEM((span, width), jnp.float32),
        ],
        compiler_params=pltpu.CompilerParams(vmem_limit_bytes=56 * 2**20),
    )(windows, q, do, k, kt, v)


def shards(query, key_new, value_new, key_old, value_old, offset, windows, grad_out):
    head_count = lax.axis_size("head")
    seq_count = lax.axis_size("seq")
    seq_rank = lax.axis_index("seq")
    rows, all_heads, width = query.shape
    tokens = rows * head_count
    total = tokens * seq_count
    groups = key_new.shape[1]
    span = total + tokens
    shift = offset[0]

    def to_heads(x):
        x = x.transpose(1, 0, 2).reshape(head_count, all_heads // head_count, rows, width)
        return lax.all_to_all(x, "head", split_axis=0, concat_axis=0, tiled=True)

    kv = jnp.stack([key_old, value_old, key_new, value_new]).transpose(0, 2, 1, 3)
    every = lax.all_gather(kv, "seq", axis=2, tiled=True)
    q, do = to_heads(query), to_heads(grad_out)
    old = jnp.concatenate([every[:2], every[:2]], axis=2)
    line = jnp.concatenate([lax.dynamic_slice_in_dim(old, shift, total, 2), every[2:]], axis=2)
    seen = lax.dynamic_slice_in_dim(line, seq_rank * tokens, span, 2)
    dq, dk, dv = band(windows, q, do, seen[0], seen[0].transpose(0, 2, 1), seen[1], total)
    dq = lax.all_to_all(dq, "head", split_axis=0, concat_axis=0, tiled=True)
    grad_query = dq.reshape(all_heads, rows, width).transpose(1, 0, 2).astype(jnp.float32)

    line = jnp.zeros((2, groups, 2 * total, width), jnp.bfloat16)
    line = lax.dynamic_update_slice_in_dim(line, jnp.stack([dk, dv]), seq_rank * tokens, 2)
    old = line[:, :, :total]
    old = lax.dynamic_slice_in_dim(
        jnp.concatenate([old, old], axis=2), lax.rem(total - shift, total), total, 2
    )
    terms = jnp.stack([old, line[:, :, total:]])
    terms = terms.reshape(4, groups, seq_count, tokens, width).transpose(2, 0, 1, 3, 4)
    terms = lax.all_to_all(terms, "seq", split_axis=0, concat_axis=0, tiled=True)
    grads = jnp.sum(terms.astype(jnp.float32), axis=0).transpose(0, 2, 1, 3)
    return (grad_query, grads[2], grads[3], grads[0], grads[1])


def solution(mesh):
    tokens = P(("seq", "head"), None, None)
    slots = P("seq", "head", None)
    return jax.shard_map(
        shards,
        mesh=mesh,
        in_specs=(tokens, slots, slots, slots, slots, P(), P("head"), tokens),
        out_specs=(tokens, slots, slots, slots, slots),
        check_vma=False,
    )
```

time: 264 us -> 145 us (0.55)
  the two profiles are of different devices: /device:TPU:1 before, /device:TPU:0 now
where the time goes in v1:
time: 145 us
  waiting for transfers between devices  72.4 us (50%)
  Pallas kernels  18.3 us (13%)
  local copies, waits for them, and re-layouts  17.3 us (12%)
  starting transfers between devices  17.2 us (12%)
  between operations  14.9 us (10%)
  other arithmetic  4.7 us (3%)
    all_to_all x2, waiting for transfers between devices, to_heads(): return lax.all_to_all(x, 'head', split_axis=0, concat_axis=0, tiled=True)  31.8 us
    all_to_all x1, waiting for transfers between devices, shards(): lax.all_to_all(terms, 'seq', split_axis=0, concat_axis=0, tiled=True)  24.3 us
    pallas_call x1, Pallas kernels, band(): pl.pallas_call(functools.partial(band_kernel, heads, reach), grid=(groups...  18.3 us
    all_to_all x1, waiting for transfers between devices, shards(): dq = lax.all_to_all(dq, 'head', split_axis=0, concat_axis=0, tiled=True)  16.3 us
    all_to_all x2, starting transfers between devices, to_heads(): return lax.all_to_all(x, 'head', split_axis=0, concat_axis=0, tiled=True)  9.84 us
    unnamed x14, local copies, waits for them, and re-layouts  3.93 us
    all_to_all x1, starting transfers between devices, shards(): lax.all_to_all(terms, 'seq', split_axis=0, concat_axis=0, tiled=True)  3.72 us
    all_to_all x1, starting transfers between devices, shards(): dq = lax.all_to_all(dq, 'head', split_axis=0, concat_axis=0, tiled=True)  3.64 us
  transfers between devices with their start and end apart: 5, of which 4 were waited for; matrix products, arithmetic and copies ran while one was open for 10% of the time, Pallas kernels for 0%

profile of v1, /device:TPU:0, one launch (start us, length us, event | category | flops | bytes accessed | tf_op | source)
XLA Modules:
  0.0 144.8 jit_solution(7445892098929473054)
XLA Ops:
  7.2 0.0 all-gather.2.cloned.1.call-start
  7.2 0.9 copy_bitcast_fusion.1
  8.1 0.0 copy-start.2
  8.1 1.0 copy_bitcast_fusion.3
  9.1 0.7 maximum_bitcast_fusion
  9.8 0.0 all-gather.2.cloned.1.call-update
  9.8 2.3 %copy.34 = bf16[96,32,128]{2,1,0:T(8,128)(2,1)} copy(bf16[96,32,128]{2,0,1:T(8,128)(2,1)} %bitcast.53) | data formatting | bytes 1572864 | tf_op jit(solution)/shard_map/transpose | solution.py:120
  12.2 6.3 %all-to-all-start = ((bf16[4,24,32,128]{3,2,1,0:T(8,128)(2,1)}), bf16[4,24,32,128]{3,2,1,0:T(8,128)(2,1)S(1)}, u32[]{:S(2)}, u32[]{:S(2)}) async-start(bf16[4,24,32,128]{3,2,1,0:T(8,128)(2,1)} %bitcast.1), calls=%async_computation | async-start | bytes 1572864 | tf_op jit(solution)/shard_map/all_to_all | solution.py:121
  19.2 0.0 copy-done.2
  19.2 1.2 copy.35
  20.4 18.2 %all-to-all-done.q_ref = bf16[4,24,32,128]{3,2,1,0:T(8,128)(2,1)S(1)} async-done(((bf16[4,24,32,128]{3,2,1,0:T(8,128)(2,1)}), bf16[4,24,32,128]{3,2,1,0:T(8,128)(2,1)S(1)}, u32[]{:S(2)}, u32[]{:S(2)}) %all-to-all-start) | async-done | bytes 786464 | tf_op jit(solution)/shard_map/all_to_all | solution.py:121
  38.6 0.0 copy-start
  38.6 3.5 %all-to-all-start.1 = ((bf16[4,24,32,128]{3,2,1,0:T(8,128)(2,1)}), bf16[4,24,32,128]{3,2,1,0:T(8,128)(2,1)S(1)}, u32[]{:S(2)}, u32[]{:S(2)}) async-start(bf16[4,24,32,128]{3,2,1,0:T(8,128)(2,1)} %bitcast.3), calls=%async_computation.1 | async-start | bytes 1572864 | tf_op jit(solution)/shard_map/all_to_all | solution.py:121
  42.1 0.0 all-gather.2.cloned.1.call-done
  42.2 1.7 %fusion.5 = (bf16[2,2,1024,128]{3,2,1,0:T(8,128)(2,1)S(1)}, bf16[2,2,1024,128]{3,2,1,0:T(8,128)(2,1)S(1)}) fusion(bf16[4,2,1024,128]{3,2,1,0:T(8,128)(2,1)} %all-gather.2.cloned.1.call-done), kind=kLoop, calls=%fused_computation.29 | loop fusion | bytes 4194304 | tf_op jit(solution)/shard_map/slice | solution.py:127
  43.9 0.0 copy-done
  43.9 1.0 fusion.3
  44.9 0.9 fusion
  45.8 1.2 slice_bitcast_fusion.1
  47.1 1.1 copy.40.kt_ref
  48.2 13.6 %all-to-all-done.1.do_ref = bf16[4,24,32,128]{3,2,1,0:T(8,128)(2,1)S(1)} async-done(((bf16[4,24,32,128]{3,2,1,0:T(8,128)(2,1)}), bf16[4,24,32,128]{3,2,1,0:T(8,128)(2,1)S(1)}, u32[]{:S(2)}, u32[]{:S(2)}) %all-to-all-start.1) | async-done | bytes 786464 | tf_op jit(solution)/shard_map/all_to_all | solution.py:121
  61.8 0.0 copy-start.1
  61.8 0.9 copy-done.1
  62.6 18.3 %shard_map.119 = (bf16[4,24,32,128]{3,2,1,0:T(8,128)(2,1)}, bf16[2,1152,128]{2,1,0:T(8,128)(2,1)}, bf16[2,1152,128]{2,1,0:T(8,128)(2,1)}) custom-call(s32[2]{0:T(128)} %win_ref.1, bf16[4,24,32,128]{3,2,1,0:T(8,128)(2,1)} %copy-done, bf16[4,24,32,128]{3,2,1,0:T(8,128)(2,1)} %copy-done.1, bf16[2,1152,128]{2,1,0:T(8,128)(2,1)} %get-tuple-element.27.k_ref, ...), custom_call_target="tpu_custom_call" | custom-call | tf_op jit(solution)/shard_map/pallas_call | solution.py:82
  80.9 0.0 copy-start.3
  80.9 0.0 copy-start.4
  80.9 3.6 %all-to-all-start.2 = ((bf16[4,24,32,128]{3,2,1,0:T(8,128)(2,1)}), bf16[4,24,32,128]{3,2,1,0:T(8,128)(2,1)S(1)}, u32[]{:S(2)}, u32[]{:S(2)}) async-start(bf16[4,24,32,128]{3,2,1,0:T(8,128)(2,1)} %get-tuple-element.8), calls=%async_computation.2 | async-start | bytes 1572864 | tf_op jit(solution)/shard_map/all_to_all | solution.py:130
  84.6 0.3 broadcast_in_dim.3
  84.8 0.0 copy-done.3
  84.9 0.0 copy-done.4
  84.9 0.2 maximum_dynamic-update-slice_fusion
  85.0 0.1 fusion.4
  85.2 1.0 fusion.2
  86.2 0.2 pad_maximum_fusion
  86.4 1.5 %copy.42 = bf16[8,4,2,128,128]{4,3,2,1,0:T(8,128)(2,1)} copy(bf16[8,4,2,128,128]{4,3,0,2,1:T(8,128)(2,1)S(1)} %bitcast.50) | data formatting | bytes 4194304 | tf_op jit(solution)/shard_map/transpose | solution.py:140
  87.9 16.3 %all-to-all-done.2 = bf16[4,24,32,128]{3,2,1,0:T(8,128)(2,1)S(1)} async-done(((bf16[4,24,32,128]{3,2,1,0:T(8,128)(2,1)}), bf16[4,24,32,128]{3,2,1,0:T(8,128)(2,1)S(1)}, u32[]{:S(2)}, u32[]{:S(2)}) %all-to-all-start.2) | async-done | bytes 786464 | tf_op jit(solution)/shard_map/all_to_all | solution.py:130
  104.2 3.7 %all-to-all-start.3 = ((bf16[8,4,2,128,128]{4,3,2,1,0:T(8,128)(2,1)}), bf16[8,4,2,128,128]{4,3,2,1,0:T(8,128)(2,1)S(1)}, u32[]{:S(2)}, u32[]{:S(2)}) async-start(bf16[8,4,2,128,128]{4,3,2,1,0:T(8,128)(2,1)} %copy.42), calls=%async_computation.3 | async-start | bytes 4194304 | tf_op jit(solution)/shard_map/all_to_all | solution.py:141
  107.9 0.3 bitcast_convert_fusion
  108.2 2.1 %copy.54 = f32[96,32,128]{2,0,1:T(8,128)} copy(f32[96,32,128]{2,1,0:T(8,128)S(1)} %bitcast_convert_fusion) | data formatting | bytes 3145728 | tf_op jit(solution)/shard_map/convert_element_type | solution.py:131
  110.2 24.3 %all-to-all-done.3 = bf16[8,4,2,128,128]{4,3,2,1,0:T(8,128)(2,1)S(1)} async-done(((bf16[8,4,2,128,128]{4,3,2,1,0:T(8,128)(2,1)}), bf16[8,4,2,128,128]{4,3,2,1,0:T(8,128)(2,1)S(1)}, u32[]{:S(2)}, u32[]{:S(2)}) %all-to-all-start.3) | async-done | bytes 2097184 | tf_op jit(solution)/shard_map/all_to_all | solution.py:141
  134.5 0.3 convert_reduce_fusion
  134.9 0.8 copy.44
  135.7 0.8 copy.45
  136.4 0.8 copy.46
  137.2 0.8 copy.47
  (1 shorter events, 0.0 us)
Async XLA Ops:
  7.2 35.0 %all-gather.2.cloned.1.call-start = ((), (), s32[]{:S(2)}) async-start(), calls=%async_computation.4 | async-start | bytes 2359296 | tf_op jit(solution)/shard_map/all_gather | solution.py:124
  8.1 11.1 %copy-start.2 = (bf16[32,96,128]{2,1,0:T(8,128)(2,1)S(1)}, bf16[32,96,128]{2,1,0:T(8,128)(2,1)}, u32[]{:S(2)}) copy-start(bf16[32,96,128]{2,1,0:T(8,128)(2,1)} %param.15) | copy-start | bytes 2359300
  12.2 26.5 %all-to-all-start = ((bf16[4,24,32,128]{3,2,1,0:T(8,128)(2,1)}), bf16[4,24,32,128]{3,2,1,0:T(8,128)(2,1)S(1)}, u32[]{:S(2)}, u32[]{:S(2)}) async-start(bf16[4,24,32,128]{3,2,1,0:T(8,128)(2,1)} %bitcast.1), calls=%async_computation | async-start | bytes 1572864 | tf_op jit(solution)/shard_map/all_to_all | solution.py:121
  38.6 5.2 %copy-start = (bf16[4,24,32,128]{3,2,1,0:T(8,128)(2,1)}, bf16[4,24,32,128]{3,2,1,0:T(8,128)(2,1)S(1)}, u32[]{:S(2)}) copy-start(bf16[4,24,32,128]{3,2,1,0:T(8,128)(2,1)S(1)} %all-to-all-done.q_ref) | copy-start | bytes 2359300
  38.6 23.1 %all-to-all-start.1 = ((bf16[4,24,32,128]{3,2,1,0:T(8,128)(2,1)}), bf16[4,24,32,128]{3,2,1,0:T(8,128)(2,1)S(1)}, u32[]{:S(2)}, u32[]{:S(2)}) async-start(bf16[4,24,32,128]{3,2,1,0:T(8,128)(2,1)} %bitcast.3), calls=%async_computation.1 | async-start | bytes 1572864 | tf_op jit(solution)/shard_map/all_to_all | solution.py:121
  61.8 0.9 copy-start.1
  80.9 3.9 %copy-start.3 = (bf16[2,1152,128]{2,1,0:T(8,128)(2,1)S(1)}, bf16[2,1152,128]{2,1,0:T(8,128)(2,1)}, u32[]{:S(2)}) copy-start(bf16[2,1152,128]{2,1,0:T(8,128)(2,1)} %get-tuple-element.9) | copy-start | bytes 1769476
  80.9 4.0 %copy-start.4 = (bf16[2,1152,128]{2,1,0:T(8,128)(2,1)S(1)}, bf16[2,1152,128]{2,1,0:T(8,128)(2,1)}, u32[]{:S(2)}) copy-start(bf16[2,1152,128]{2,1,0:T(8,128)(2,1)} %get-tuple-element.10) | copy-start | bytes 1769476
  80.9 23.3 %all-to-all-start.2 = ((bf16[4,24,32,128]{3,2,1,0:T(8,128)(2,1)}), bf16[4,24,32,128]{3,2,1,0:T(8,128)(2,1)S(1)}, u32[]{:S(2)}, u32[]{:S(2)}) async-start(bf16[4,24,32,128]{3,2,1,0:T(8,128)(2,1)} %get-tuple-element.8), calls=%async_computation.2 | async-start | bytes 1572864 | tf_op jit(solution)/shard_map/all_to_all | solution.py:130
  104.2 30.3 %all-to-all-start.3 = ((bf16[8,4,2,128,128]{4,3,2,1,0:T(8,128)(2,1)}), bf16[8,4,2,128,128]{4,3,2,1,0:T(8,128)(2,1)S(1)}, u32[]{:S(2)}, u32[]{:S(2)}) async-start(bf16[8,4,2,128,128]{4,3,2,1,0:T(8,128)(2,1)} %copy.42), calls=%async_computation.3 | async-start | bytes 4194304 | tf_op jit(solution)/shard_map/all_to_all | solution.py:141
Sparse Core Ops, SparseCore 0:
  10.0 30.4 all-gather.1

commit v2 on v1

v2 whole, which is shorter than its diff:
```python
import functools
import math

import jax
import jax.numpy as jnp
from jax import lax
from jax.experimental import pallas as pl
from jax.experimental.pallas import tpu as pltpu
from jax.sharding import PartitionSpec as P

MESH = pl.DeviceIdType.MESH
NT = (((1,), (1,)), ((), ()))
NN = (((1,), (0,)), ((), ()))


def dot(a, b, dims):
    return lax.dot_general(a, b, dims, preferred_element_type=jnp.float32)


def kernel(
    heads, seqs, per_group, heads_at_once,
    win_ref, off_ref, q_ref, do_ref, kv_ref,
    dq_ref, grad_ref,
    q_all, do_all, kv_all, line, keys_t, bias, sums, terms, term_out, term_in, dq_out, dq_in,
    q_send, q_recv, do_send, do_recv, kv_send, kv_recv, dq_send, dq_recv, old_send, old_recv, new_send, new_recv,
):
    hb = heads_at_once
    me_h, me_s = lax.axis_index("head"), lax.axis_index("seq")
    rows, width = q_ref.shape[2:]
    tokens = rows * heads
    groups = q_ref.shape[1] // per_group
    total = tokens * seqs
    span = total + tokens
    steps = per_group // hb
    chunks = groups * steps
    scale = 1.0 / math.sqrt(width)
    pair = 2 * width

    def peer_h(k):
        return lax.rem(me_h + k, heads)

    def peer_s(k):
        return lax.rem(me_s + k, seqs)

    def row_copy(src, dst, send, recv, chunk, there, slot):
        part = pl.ds(chunk * hb, hb)
        return pltpu.make_async_remote_copy(
            src_ref=src.at[there, part], dst_ref=dst.at[slot, part],
            send_sem=send.at[chunk, there], recv_sem=recv.at[chunk, slot],
            device_id={"head": there}, device_id_type=MESH,
        )

    def kv_copy(there, slot):
        return pltpu.make_async_remote_copy(
            src_ref=kv_ref, dst_ref=kv_all.at[slot],
            send_sem=kv_send.at[there], recv_sem=kv_recv.at[slot],
            device_id={"seq": there}, device_id_type=MESH,
        )

    def term_copy(group, kind, there, slot):
        send, recv = ((old_send, old_recv), (new_send, new_recv))[kind]
        return pltpu.make_async_remote_copy(
            src_ref=term_out.at[group, kind, there], dst_ref=term_in.at[group, kind, slot],
            send_sem=send.at[group, there], recv_sem=recv.at[group, slot],
            device_id={"seq": there}, device_id_type=MESH,
        )

    barrier = pltpu.get_barrier_semaphore()
    for k in range(1, heads):
        pl.semaphore_signal(barrier, inc=1, device_id={"head": peer_h(k)}, device_id_type=MESH)
    for k in range(1, seqs):
        pl.semaphore_signal(barrier, inc=1, device_id={"seq": peer_s(k)}, device_id_type=MESH)
    pl.semaphore_wait(barrier, heads + seqs - 2)

    @pl.loop(1, seqs)
    def _(k):
        kv_copy(peer_s(k), me_s).start()

    @pl.loop(0, chunks)
    def _(chunk):
        for k in range(1, heads):
            row_copy(q_ref, q_all, q_send, q_recv, chunk, peer_h(k), me_h).start()
            row_copy(do_ref, do_all, do_send, do_recv, chunk, peer_h(k), me_h).start()

    q_all[me_h] = q_ref[me_h]
    do_all[me_h] = do_ref[me_h]
    kv_all[me_s] = kv_ref[...]

    @pl.loop(1, seqs)
    def _(k):
        kv_copy(peer_s(k), peer_s(k)).wait_recv()

    base = lax.rem(off_ref[0] + me_s * tokens, total)
    old_rows = total - me_s * tokens

    def slot_of(row):
        slot = row + base
        return jnp.where(slot >= total, slot - total, slot)

    @pl.loop(0, seqs - me_s)
    def _(block):
        row = block * tokens + lax.broadcasted_iota(jnp.int32, (tokens, total), 0)
        slot = lax.broadcasted_iota(jnp.int32, (tokens, total), 1)
        pick = jnp.where(slot_of(row) == slot, 1.0, 0.0).astype(jnp.bfloat16)
        stored = kv_all[:, 0].reshape(total, groups * pair)
        line[pl.ds(block * tokens, tokens)] = dot(pick, stored, NN).astype(jnp.bfloat16)

    @pl.loop(0, me_s + 1)
    def _(block):
        line[pl.ds((seqs - me_s + block) * tokens, tokens)] = kv_all[block, 1]

    for group in range(groups):
        left = group * pair
        window = win_ref[group]
        place = lax.broadcasted_iota(jnp.int32, (span, tokens), 0) - total
        token = lax.broadcasted_iota(jnp.int32, (span, tokens), 1)
        bias[...] = jnp.where((place <= token) & (place > token - window), 0.0, -jnp.inf)
        keys_t[...] = line[:, left : left + width].T
        sums[...] = jnp.zeros_like(sums)

        @pl.loop(0, steps)
        def _(step):
            chunk = group * steps + step
            first = chunk * hb
            for k in range(1, heads):
                row_copy(q_ref, q_all, q_send, q_recv, chunk, peer_h(k), peer_h(k)).wait_recv()
                row_copy(do_ref, do_all, do_send, do_recv, chunk, peer_h(k), peer_h(k)).wait_recv()
            q = jnp.concatenate([q_all[:, first + h].reshape(tokens, width) for h in range(hb)], 0)
            do = jnp.concatenate([do_all[:, first + h].reshape(tokens, width) for h in range(hb)], 0)
            keys = line[:, left : left + width]
            values = line[:, left + width : left + pair]
            scores = dot(keys, q, NT) + jnp.concatenate([bias[...]] * hb, 1)
            top = jnp.max(scores, axis=0, keepdims=True)
            grown = jnp.exp2((scores - top) * (scale * math.log2(math.e)))
            inverse = 1.0 / jnp.sum(grown, axis=0, keepdims=True)
            weight_grad = dot(values, do, NT)
            delta = jnp.sum(grown * weight_grad, axis=0, keepdims=True) * inverse
            weights = grown * inverse
            dscore = (weights * (weight_grad - delta)).astype(jnp.bfloat16)
            dqt = dot(keys_t[...], dscore, NN) * scale
            for h in range(hb):
                piece = dqt[:, h * tokens : (h + 1) * tokens].T.astype(jnp.bfloat16)
                dq_out[:, first + h] = piece.reshape(heads, rows, width)
            for k in range(1, heads):
                row_copy(dq_out, dq_in, dq_send, dq_recv, chunk, peer_h(k), me_h).start()
            sums[:, :width] += dot(dscore, q, NN)
            sums[:, width:] += dot(weights.astype(jnp.bfloat16), do, NN)

        terms[:, :width] = (sums[:, :width] * scale).astype(jnp.bfloat16)
        terms[:, width:] = sums[:, width:].astype(jnp.bfloat16)

        @pl.loop(0, seqs)
        def _(k):
            there = peer_s(k)
            row = lax.broadcasted_iota(jnp.int32, (tokens, total), 1)
            slot = there * tokens + lax.broadcasted_iota(jnp.int32, (tokens, total), 0)
            chosen = (slot_of(row) == slot) & (row < old_rows)
            pick = jnp.where(chosen, 1.0, 0.0).astype(jnp.bfloat16)
            term_out[group, 0, there] = dot(pick, terms[:total], NN).astype(jnp.bfloat16)

            @pl.when(there <= me_s)
            def _():
                term_out[group, 1, there] = terms[pl.ds((seqs - me_s + there) * tokens, tokens)]

            @pl.when(k > 0)
            def _():
                term_copy(group, 0, there, me_s).start()

                @pl.when(there < me_s)
                def _():
                    term_copy(group, 1, there, me_s).start()

    for k in range(heads):
        there = peer_h(k)
        place = pl.ds(there * groups * per_group, groups * per_group)
        if k == 0:
            dq_ref[place] = dq_out[there].astype(jnp.float32)
            continue

        @pl.loop(0, chunks)
        def _(chunk):
            row_copy(dq_out, dq_in, dq_send, dq_recv, chunk, there, there).wait_recv()

        dq_ref[place] = dq_in[there].astype(jnp.float32)

    for group in range(groups):
        for kind in range(2):
            grad_ref[group, kind] = term_out[group, kind, me_s].astype(jnp.float32)

        @pl.loop(1, seqs)
        def _(k):
            there = peer_s(k)
            term_copy(group, 0, there, there).wait_recv()
            grad_ref[group, 0] += term_in[group, 0, there].astype(jnp.float32)

            @pl.when(there > me_s)
            def _():
                term_copy(group, 1, there, there).wait_recv()
                grad_ref[group, 1] += term_in[group, 1, there].astype(jnp.float32)

    @pl.loop(0, chunks)
    def _(chunk):
        for k in range(1, heads):
            row_copy(q_ref, q_all, q_send, q_recv, chunk, peer_h(k), me_h).wait_send()
            row_copy(do_ref, do_all, do_send, do_recv, chunk, peer_h(k), me_h).wait_send()
            row_copy(dq_out, dq_in, dq_send, dq_recv, chunk, peer_h(k), me_h).wait_send()

    @pl.loop(1, seqs)
    def _(k):
        there = peer_s(k)
        kv_copy(there, me_s).wait_send()
        for group in range(groups):
            term_copy(group, 0, there, me_s).wait_send()

            @pl.when(there < me_s)
            def _():
                term_copy(group, 1, there, me_s).wait_send()


def shards(query, key_new, value_new, key_old, value_old, offset, windows, grad_out):
    heads, seqs = lax.axis_size("head"), lax.axis_size("seq")
    rows, all_heads, width = query.shape
    tokens = rows * heads
    total = tokens * seqs
    groups = key_new.shape[1]
    span = total + tokens
    mine = all_heads // heads
    per_group = mine // groups
    hb = max(h for h in (1, 2, 4) if per_group % h == 0 and (h <= 1 or h * tokens * span <= 700_000))
    chunks = mine // hb

    def by_head(x):
        return x.transpose(1, 0, 2).reshape(heads, mine, rows, width)

    kv = jnp.stack([jnp.stack([key_old, value_old], 2), jnp.stack([key_new, value_new], 2)])
    kv = kv.reshape(2, tokens, groups * 2 * width)
    vmem = pl.BlockSpec(memory_space=pltpu.VMEM)
    smem = pl.BlockSpec(memory_space=pltpu.SMEM)
    narrow, wide = jnp.bfloat16, jnp.float32
    row_shape = (heads, mine, rows, width)
    row_sems = pltpu.SemaphoreType.DMA((chunks, heads))
    seq_sems = pltpu.SemaphoreType.DMA((seqs,))
    term_sems = pltpu.SemaphoreType.DMA((groups, seqs))
    term_shape = (groups, 2, seqs, tokens, 2 * width)
    dq, grads = pl.pallas_call(
        functools.partial(kernel, heads, seqs, per_group, hb),
        in_specs=[smem, smem, vmem, vmem, vmem],
        out_specs=[vmem, vmem],
        out_shape=[
            jax.ShapeDtypeStruct((all_heads, rows, width), wide),
            jax.ShapeDtypeStruct((groups, 2, tokens, 2 * width), wide),
        ],
        scratch_shapes=[
            pltpu.VMEM(row_shape, narrow),
            pltpu.VMEM(row_shape, narrow),
            pltpu.VMEM((seqs, 2, tokens, groups * 2 * width), narrow),
            pltpu.VMEM((span, groups * 2 * width), narrow),
            pltpu.VMEM((width, span), narrow),
            pltpu.VMEM((span, tokens), wide),
            pltpu.VMEM((span, 2 * width), wide),
            pltpu.VMEM((span, 2 * width), narrow),
            pltpu.VMEM(term_shape, narrow),
            pltpu.VMEM(term_shape, narrow),
            pltpu.VMEM(row_shape, narrow),
            pltpu.VMEM(row_shape, narrow),
            row_sems, row_sems, row_sems, row_sems, seq_sems, seq_sems,
            row_sems, row_sems, term_sems, term_sems, term_sems, term_sems,
        ],
        compiler_params=pltpu.CompilerParams(
            collective_id=0, has_side_effects=True, vmem_limit_bytes=62 * 2**20
        ),
    )(windows, offset, by_head(query), by_head(grad_out), kv)
    grad_query = dq.transpose(1, 0, 2)
    grads = grads.reshape(groups, 2, tokens, 2, width).transpose(1, 3, 2, 0, 4)
    return (grad_query, grads[1, 0], grads[1, 1], grads[0, 0], grads[0, 1])


def solution(mesh):
    tokens = P(("seq", "head"), None, None)
    slots = P("seq", "head", None)
    return jax.shard_map(
        shards,
        mesh=mesh,
        in_specs=(tokens, slots, slots, slots, slots, P(), P("head"), tokens),
        out_specs=(tokens, slots, slots, slots, slots),
        check_vma=False,
    )
```

time: 145 us -> 78.1 us (0.54)
  the two profiles are of different devices: /device:TPU:0 before, /device:TPU:1 now
where the time goes in v2:
time: 78.1 us; the launch traced here: 77.9 us
  Pallas kernels  65.6 us (84%)
  local copies, waits for them, and re-layouts  7.93 us (10%)
  other arithmetic  2.94 us (4%)
  between operations  1.43 us (2%)
    pallas_call x1, Pallas kernels, shards(): pl.pallas_call(functools.partial(kernel, heads, seqs, per_group, hb), in_...  65.6 us
    unnamed x7, local copies, waits for them, and re-layouts  3.54 us
    transpose x2, local copies, waits for them, and re-layouts, by_head(): return x.transpose(1, 0, 2).reshape(heads, mine, rows, width)  2.39 us

profile of v2, /device:TPU:1, one launch (start us, length us, event | category | flops | bytes accessed | tf_op | source)
XLA Modules:
  0.0 77.9 jit_solution(11104057496742007233)
XLA Ops:
  0.6 0.0 copy-start
  1.4 1.1 %pad_maximum_fusion.2 = bf16[128,2,2,128]{3,1,0,2:T(2,128)(2,1)S(1)} fusion(bf16[128,2,1,128]{3,1,0,2:T(2,128)(2,1)} %bitcast.28, bf16[128,2,1,128]{3,1,0,2:T(2,128)(2,1)} %bitcast.29), kind=kLoop, calls=%fused_computation.7 | loop fusion | flops 65536 | bytes 262144 | tf_op jit(solution)/shard_map/stack | solution.py:235
  2.4 0.2 copy.16
  2.6 0.0 copy-start.1
  2.7 0.1 stack.34
  2.7 1.1 %pad_maximum_fusion.1 = bf16[128,2,2,128]{3,1,0,2:T(2,128)(2,1)S(1)} fusion(bf16[128,2,1,128]{3,1,0,2:T(2,128)(2,1)} %bitcast.30, bf16[128,2,1,128]{3,1,0,2:T(2,128)(2,1)} %bitcast.31), kind=kLoop, calls=%fused_computation.6 | loop fusion | flops 65536 | bytes 262144 | tf_op jit(solution)/shard_map/stack | solution.py:235
  3.8 0.2 copy.15
  4.1 0.1 stack.30
  4.1 0.7 pad_maximum_fusion.kv_ref
  4.9 0.0 copy-done
  4.9 1.2 %copy.13 = bf16[96,32,128]{2,1,0:T(8,128)(2,1)} copy(bf16[96,32,128]{2,0,1:T(8,128)(2,1)S(1)} %bitcast.26) | data formatting | bytes 1572864 | tf_op jit(solution)/shard_map/transpose | solution.py:233
  6.1 0.0 copy-done.1
  6.1 1.2 %copy.14 = bf16[96,32,128]{2,1,0:T(8,128)(2,1)} copy(bf16[96,32,128]{2,0,1:T(8,128)(2,1)S(1)} %bitcast.27) | data formatting | bytes 1572864 | tf_op jit(solution)/shard_map/transpose | solution.py:233
  7.3 65.6 %shard_map.119 = (f32[96,32,128]{2,1,0:T(8,128)}, f32[2,2,128,256]{3,2,1,0:T(8,128)}) custom-call(s32[2]{0:T(128)} %win_ref.1, s32[1]{0:T(128)S(6)} %copy.21.off_ref, bf16[4,24,32,128]{3,2,1,0:T(8,128)(2,1)} %bitcast.22, bf16[4,24,32,128]{3,2,1,0:T(8,128)(2,1)} %bitcast.23, bf16[2,128,512]{2,1,0:T(8,128)(2,1)} %pad_maximum_fusion.kv_ref), custom_call_target="tpu_custom_call" | custom-call | tf_op jit(solution)/shard_map/pallas_call | solution.py:245
  72.9 0.0 copy-start.2
  72.9 3.5 %copy.18 = f32[32,96,128]{2,1,0:T(8,128)} copy(f32[32,96,128]{2,0,1:T(8,128)} %bitcast.25) | data formatting | bytes 3145728
  76.4 0.0 copy-done.2
  76.4 0.3 reshape.26
  76.7 0.4 copy.20
  77.1 0.8 %slice_bitcast_fusion = (f32[128,2,128]{2,1,0:T(2,128)}, f32[128,2,128]{2,1,0:T(2,128)}, f32[128,2,128]{2,1,0:T(2,128)}, f32[128,2,128]{2,1,0:T(2,128)}) fusion(f32[2,2,128,2,128]{4,3,2,1,0:T(2,128)S(1)} %bitcast.24), kind=kLoop, calls=%fused_computation.2 | loop fusion | bytes 1048576 | tf_op jit(solution)/shard_map/squeeze | solution.py:275
Async XLA Ops:
  0.6 4.2 %copy-start = (bf16[32,96,128]{2,1,0:T(8,128)(2,1)S(1)}, bf16[32,96,128]{2,1,0:T(8,128)(2,1)}, u32[]{:S(2)}) copy-start(bf16[32,96,128]{2,1,0:T(8,128)(2,1)} %param.8) | copy-start | bytes 2359300
  2.6 3.4 %copy-start.1 = (bf16[32,96,128]{2,1,0:T(8,128)(2,1)S(1)}, bf16[32,96,128]{2,1,0:T(8,128)(2,1)}, u32[]{:S(2)}) copy-start(bf16[32,96,128]{2,1,0:T(8,128)(2,1)} %param.15) | copy-start | bytes 2359300
  72.9 3.5 %copy-start.2 = (f32[2,2,128,256]{3,2,1,0:T(8,128)S(1)}, f32[2,2,128,256]{3,2,1,0:T(8,128)}, u32[]{:S(2)}) copy-start(f32[2,2,128,256]{3,2,1,0:T(8,128)} %get-tuple-element.8) | copy-start | bytes 1572868

commit v3 on v2

--- a/solution.py
+++ b/solution.py
@@ -19,10 +19,10 @@
 
 def kernel(
     heads, seqs, per_group, heads_at_once,
-    win_ref, off_ref, q_ref, do_ref, kv_ref,
+    win_ref, off_ref, q_ref, do_ref, ko_ref, vo_ref, kn_ref, vn_ref,
     dq_ref, grad_ref,
     q_all, do_all, kv_all, line, keys_t, bias, sums, terms, term_out, term_in, dq_out, dq_in,
-    q_send, q_recv, do_send, do_recv, kv_send, kv_recv, dq_send, dq_recv, old_send, old_recv, new_send, new_recv,
+    q_send, q_recv, do_send, do_recv, kv_send, kv_recv, pass_send, dq_send, dq_recv, old_send, old_recv, new_send, new_recv,
 ):
     hb = heads_at_once
     me_h, me_s = lax.axis_index("head"), lax.axis_index("seq")
@@ -34,7 +34,6 @@
     steps = per_group // hb
     chunks = groups * steps
     scale = 1.0 / math.sqrt(width)
-    pair = 2 * width
 
     def peer_h(k):
         return lax.rem(me_h + k, heads)
@@ -52,9 +51,18 @@
 
     def kv_copy(there, slot):
         return pltpu.make_async_remote_copy(
-            src_ref=kv_ref, dst_ref=kv_all.at[slot],
+            src_ref=kv_all.at[me_s], dst_ref=kv_all.at[slot],
             send_sem=kv_send.at[there], recv_sem=kv_recv.at[slot],
             device_id={"seq": there}, device_id_type=MESH,
+        )
+
+    partner = me_s + 1 - 2 * lax.rem(me_s, 2)
+
+    def pass_copy(slot):
+        return pltpu.make_async_remote_copy(
+            src_ref=kv_all.at[slot], dst_ref=kv_all.at[slot],
+            send_sem=pass_send.at[slot], recv_sem=kv_recv.at[slot],
+            device_id={"seq": partner}, device_id_type=MESH,
         )
 
     def term_copy(group, kind, there, slot):
@@ -65,6 +73,9 @@
             device_id={"seq": there}, device_id_type=MESH,
         )
 
+    for kind, ref in enumerate((ko_ref, vo_ref, kn_ref, vn_ref)):
+        kv_all[me_s, kind] = ref[...]
+
     barrier = pltpu.get_barrier_semaphore()
     for k in range(1, heads):
         pl.semaphore_signal(barrier, inc=1, device_id={"head": peer_h(k)}, device_id_type=MESH)
@@ -72,9 +83,11 @@
         pl.semaphore_signal(barrier, inc=1, device_id={"seq": peer_s(k)}, device_id_type=MESH)
     pl.semaphore_wait(barrier, heads + seqs - 2)
 
-    @pl.loop(1, seqs)
-    def _(k):
-        kv_copy(peer_s(k), me_s).start()
+    @pl.loop(1, seqs // 2)
+    def _(k):
+        kv_copy(peer_s(2 * k), me_s).start()
+
+    kv_copy(partner, me_s).start()
 
     @pl.loop(0, chunks)
     def _(chunk):
@@ -84,11 +97,17 @@
 
     q_all[me_h] = q_ref[me_h]
     do_all[me_h] = do_ref[me_h]
-    kv_all[me_s] = kv_ref[...]
-
-    @pl.loop(1, seqs)
-    def _(k):
-        kv_copy(peer_s(k), peer_s(k)).wait_recv()
+
+    @pl.loop(1, seqs // 2)
+    def _(k):
+        slot = peer_s(2 * k)
+        kv_copy(slot, slot).wait_recv()
+        pass_copy(slot).start()
+
+    @pl.loop(0, seqs // 2)
+    def _(k):
+        slot = lax.rem(partner + 2 * k, seqs)
+        kv_copy(slot, slot).wait_recv()
 
     base = lax.rem(off_ref[0] + me_s * tokens, total)
     old_rows = total - me_s * tokens
@@ -102,20 +121,22 @@
         row = block * tokens + lax.broadcasted_iota(jnp.int32, (tokens, total), 0)
         slot = lax.broadcasted_iota(jnp.int32, (tokens, total), 1)
         pick = jnp.where(slot_of(row) == slot, 1.0, 0.0).astype(jnp.bfloat16)
-        stored = kv_all[:, 0].reshape(total, groups * pair)
-        line[pl.ds(block * tokens, tokens)] = dot(pick, stored, NN).astype(jnp.bfloat16)
+        for kind in range(2):
+            stored = kv_all[:, kind].reshape(total, groups * width)
+            line[kind, pl.ds(block * tokens, tokens)] = dot(pick, stored, NN).astype(jnp.bfloat16)
 
     @pl.loop(0, me_s + 1)
     def _(block):
-        line[pl.ds((seqs - me_s + block) * tokens, tokens)] = kv_all[block, 1]
+        for kind in range(2):
+            line[kind, pl.ds((seqs - me_s + block) * tokens, tokens)] = kv_all[block, 2 + kind]
 
     for group in range(groups):
-        left = group * pair
+        left = group * width
         window = win_ref[group]
         place = lax.broadcasted_iota(jnp.int32, (span, tokens), 0) - total
         token = lax.broadcasted_iota(jnp.int32, (span, tokens), 1)
         bias[...] = jnp.where((place <= token) & (place > token - window), 0.0, -jnp.inf)
-        keys_t[...] = line[:, left : left + width].T
+        keys_t[...] = line[0, :, left : left + width].T
         sums[...] = jnp.zeros_like(sums)
 
         @pl.loop(0, steps)
@@ -127,8 +148,8 @@
                 row_copy(do_ref, do_all, do_send, do_recv, chunk, peer_h(k), peer_h(k)).wait_recv()
             q = jnp.concatenate([q_all[:, first + h].reshape(tokens, width) for h in range(hb)], 0)
             do = jnp.concatenate([do_all[:, first + h].reshape(tokens, width) for h in range(hb)], 0)
-            keys = line[:, left : left + width]
-            values = line[:, left + width : left + pair]
+            keys = line[0, :, left : left + width]
+            values = line[1, :, left : left + width]
             scores = dot(keys, q, NT) + jnp.concatenate([bias[...]] * hb, 1)
             top = jnp.max(scores, axis=0, keepdims=True)
             grown = jnp.exp2((scores - top) * (scale * math.log2(math.e)))
@@ -174,14 +195,14 @@
         there = peer_h(k)
         place = pl.ds(there * groups * per_group, groups * per_group)
         if k == 0:
-            dq_ref[place] = dq_out[there].astype(jnp.float32)
+            dq_ref[place] = dq_out[there]
             continue
 
         @pl.loop(0, chunks)
         def _(chunk):
             row_copy(dq_out, dq_in, dq_send, dq_recv, chunk, there, there).wait_recv()
 
-        dq_ref[place] = dq_in[there].astype(jnp.float32)
+        dq_ref[place] = dq_in[there]
 
     for group in range(groups):
         for kind in range(2):
@@ -197,6 +218,13 @@
             def _():
                 term_copy(group, 1, there, there).wait_recv()
                 grad_ref[group, 1] += term_in[group, 1, there].astype(jnp.float32)
+
+    kv_copy(partner, me_s).wait_send()
+
+    @pl.loop(1, seqs // 2)
+    def _(k):
+        kv_copy(peer_s(2 * k), me_s).wait_send()
+        pass_copy(peer_s(2 * k)).wait_send()
 
     @pl.loop(0, chunks)
     def _(chunk):
@@ -208,7 +236,6 @@
     @pl.loop(1, seqs)
     def _(k):
         there = peer_s(k)
-        kv_copy(there, me_s).wait_send()
         for group in range(groups):
             term_copy(group, 0, there, me_s).wait_send()
 
@@ -232,8 +259,7 @@
     def by_head(x):
         return x.transpose(1, 0, 2).reshape(heads, mine, rows, width)
 
-    kv = jnp.stack([jnp.stack([key_old, value_old], 2), jnp.stack([key_new, value_new], 2)])
-    kv = kv.reshape(2, tokens, groups * 2 * width)
+    kv = [x.reshape(tokens, groups * width) for x in (key_old, value_old, key_new, value_new)]
     vmem = pl.BlockSpec(memory_space=pltpu.VMEM)
     smem = pl.BlockSpec(memory_space=pltpu.SMEM)
     narrow, wide = jnp.bfloat16, jnp.float32
@@ -244,17 +270,17 @@
     term_shape = (groups, 2, seqs, tokens, 2 * width)
     dq, grads = pl.pallas_call(
         functools.partial(kernel, heads, seqs, per_group, hb),
-        in_specs=[smem, smem, vmem, vmem, vmem],
+        in_specs=[smem, smem] + [vmem] * 6,
         out_specs=[vmem, vmem],
         out_shape=[
-            jax.ShapeDtypeStruct((all_heads, rows, width), wide),
+            jax.ShapeDtypeStruct((all_heads, rows, width), narrow),
             jax.ShapeDtypeStruct((groups, 2, tokens, 2 * width), wide),
         ],
         scratch_shapes=[
             pltpu.VMEM(row_shape, narrow),
             pltpu.VMEM(row_shape, narrow),
-            pltpu.VMEM((seqs, 2, tokens, groups * 2 * width), narrow),
-            pltpu.VMEM((span, groups * 2 * width), narrow),
+            pltpu.VMEM((seqs, 4, tokens, groups * width), narrow),
+            pltpu.VMEM((2, span, groups * width), narrow),
             pltpu.VMEM((width, span), narrow),
             pltpu.VMEM((span, tokens), wide),
             pltpu.VMEM((span, 2 * width), wide),
@@ -263,14 +289,14 @@
             pltpu.VMEM(term_shape, narrow),
             pltpu.VMEM(row_shape, narrow),
             pltpu.VMEM(row_shape, narrow),
-            row_sems, row_sems, row_sems, row_sems, seq_sems, seq_sems,
+            row_sems, row_sems, row_sems, row_sems, seq_sems, seq_sems, seq_sems,
             row_sems, row_sems, term_sems, term_sems, term_sems, term_sems,
         ],
         compiler_params=pltpu.CompilerParams(
             collective_id=0, has_side_effects=True, vmem_limit_bytes=62 * 2**20
         ),
-    )(windows, offset, by_head(query), by_head(grad_out), kv)
-    grad_query = dq.transpose(1, 0, 2)
+    )(windows, offset, by_head(query), by_head(grad_out), *kv)
+    grad_query = lax.optimization_barrier(dq.transpose(1, 0, 2)).astype(wide)
     grads = grads.reshape(groups, 2, tokens, 2, width).transpose(1, 3, 2, 0, 4)
     return (grad_query, grads[1, 0], grads[1, 1], grads[0, 0], grads[0, 1])
 

time: 78.1 us -> 76.9 us (0.985)
  other arithmetic: 2.94 us -> 0 us
  local copies, waits for them, and re-layouts: 7.93 us -> 10.6 us
  Pallas kernels: 65.6 us -> 64.7 us
    reshape x0 -> x2, local copies, waits for them, and re-layouts: none -> 3.07 us  [shards(): x.reshape(tokens, groups * width)]
    another operation x3 -> x0, other arithmetic: 2.94 us -> none  [the longest x1 1.13 us: shards(): jnp.stack([key_old, value_old], 2)]
    unnamed x7 -> x5, local copies, waits for them, and re-layouts: 3.54 us -> 1.41 us
    transpose x2, local copies, waits for them, and re-layouts: 2.39 us -> 3.52 us  [by_head(): return x.transpose(1, 0, 2).reshape(heads, mine, rows, width)]
    reshape x2, local copies, waits for them, and re-layouts: 0.68 us -> 1.78 us  [shards(): grads = grads.reshape(groups, 2, tokens, 2, width).transpose(1, 3, 2, 0, 4)]
    pallas_call x1, Pallas kernels: 65.6 us -> 64.7 us  [shards(): pl.pallas_call(functools.partial(kernel, heads, seqs, per_group, hb), in_...]
where the time goes in v3:
time: 76.9 us; the launch traced here: 76.6 us
  Pallas kernels  64.7 us (84%)
  local copies, waits for them, and re-layouts  10.6 us (14%)
  between operations  1.39 us (2%)
    pallas_call x1, Pallas kernels, shards(): pl.pallas_call(functools.partial(kernel, heads, seqs, per_group, hb), in_...  64.7 us
    transpose x2, local copies, waits for them, and re-layouts, by_head(): return x.transpose(1, 0, 2).reshape(heads, mine, rows, width)  3.52 us
    reshape x2, local copies, waits for them, and re-layouts, shards(): x.reshape(tokens, groups * width)  3.07 us
    reshape x2, local copies, waits for them, and re-layouts, shards(): grads = grads.reshape(groups, 2, tokens, 2, width).transpose(1, 3, 2, 0, 4)  1.78 us

profile of v3, /device:TPU:1, one launch (start us, length us, event | category | flops | bytes accessed | tf_op | source)
XLA Modules:
  0.0 76.6 jit_solution(17159907377093705415)
XLA Ops:
  0.6 0.0 copy-start
  1.4 1.5 %copy_bitcast_fusion.1 = (bf16[128,256]{1,0:T(8,128)(2,1)}, bf16[128,256]{1,0:T(8,128)(2,1)}) fusion(bf16[16,8,2,128]{3,2,1,0:T(2,128)(2,1)} %bitcast.36, bf16[16,8,2,128]{3,2,1,0:T(2,128)(2,1)} %bitcast.37), kind=kLoop, calls=%fused_computation.5 | loop fusion | bytes 262144 | tf_op jit(solution)/shard_map/reshape | solution.py:262
  2.9 1.5 %copy_bitcast_fusion.3 = (bf16[128,256]{1,0:T(8,128)(2,1)}, bf16[128,256]{1,0:T(8,128)(2,1)}) fusion(bf16[16,8,2,128]{3,2,1,0:T(2,128)(2,1)} %bitcast.38, bf16[16,8,2,128]{3,2,1,0:T(2,128)(2,1)} %bitcast.39), kind=kLoop, calls=%fused_computation.7 | loop fusion | bytes 262144 | tf_op jit(solution)/shard_map/reshape | solution.py:262
  4.4 2.3 %copy.13 = bf16[96,32,128]{2,1,0:T(8,128)(2,1)} copy(bf16[96,32,128]{2,0,1:T(8,128)(2,1)} %bitcast.33) | data formatting | bytes 1572864 | tf_op jit(solution)/shard_map/transpose | solution.py:260
  6.8 0.0 copy-done
  6.8 1.2 %copy.14 = bf16[96,32,128]{2,1,0:T(8,128)(2,1)} copy(bf16[96,32,128]{2,0,1:T(8,128)(2,1)S(1)} %bitcast.34) | data formatting | bytes 1572864 | tf_op jit(solution)/shard_map/transpose | solution.py:260
  8.0 64.7 %shard_map.119 = (bf16[96,32,128]{2,1,0:T(8,128)(2,1)}, f32[2,2,128,256]{3,2,1,0:T(8,128)}) custom-call(s32[2]{0:T(128)} %win_ref.1, s32[1]{0:T(128)S(6)} %copy.27.off_ref, bf16[4,24,32,128]{3,2,1,0:T(8,128)(2,1)} %bitcast.30, bf16[4,24,32,128]{3,2,1,0:T(8,128)(2,1)} %bitcast.31, bf16[128,256]{1,0:T(8,128)(2,1)} %get-tuple-element.21.ko_ref, ...), custom_call_target="tpu_custom_call" | custom-call | tf_op jit(solution)/shard_map/pallas_call | solution.py:271
  72.6 0.0 copy-start.1
  72.7 1.4 %reshape.37 = f32[2,2,128,2,128]{4,3,2,1,0:T(2,128)S(1)} reshape(f32[2,2,128,256]{3,2,1,0:T(8,128)} %get-tuple-element.8) | data formatting | bytes 1048576 | tf_op jit(solution)/shard_map/reshape | solution.py:300
  74.0 0.4 copy.26
  74.4 0.8 %slice_bitcast_fusion = (f32[128,2,128]{2,1,0:T(2,128)}, f32[128,2,128]{2,1,0:T(2,128)}, f32[128,2,128]{2,1,0:T(2,128)}, f32[128,2,128]{2,1,0:T(2,128)}) fusion(f32[2,2,128,2,128]{4,3,2,1,0:T(2,128)S(1)} %bitcast.32), kind=kLoop, calls=%fused_computation.1 | loop fusion | bytes 1048576 | tf_op jit(solution)/shard_map/squeeze | solution.py:301
  75.2 0.0 copy-done.1
  75.2 1.4 %copy.16 = f32[32,96,128]{2,1,0:T(8,128)} copy(bf16[32,96,128]{2,0,1:T(8,128)(2,1)S(1)} %bitcast.35) | data formatting | bytes 2359296
Async XLA Ops:
  0.6 6.1 %copy-start = (bf16[32,96,128]{2,1,0:T(8,128)(2,1)S(1)}, bf16[32,96,128]{2,1,0:T(8,128)(2,1)}, u32[]{:S(2)}) copy-start(bf16[32,96,128]{2,1,0:T(8,128)(2,1)} %param.15) | copy-start | bytes 2359300
  72.6 2.6 %copy-start.1 = (bf16[96,32,128]{2,1,0:T(8,128)(2,1)S(1)}, bf16[96,32,128]{2,1,0:T(8,128)(2,1)}, u32[]{:S(2)}) copy-start(bf16[96,32,128]{2,1,0:T(8,128)(2,1)} %get-tuple-element.7) | copy-start | bytes 2359300

commit v4 on v3

--- a/solution.py
+++ b/solution.py
@@ -20,8 +20,8 @@
 def kernel(
     heads, seqs, per_group, heads_at_once,
     win_ref, off_ref, q_ref, do_ref, ko_ref, vo_ref, kn_ref, vn_ref,
-    dq_ref, grad_ref,
-    q_all, do_all, kv_all, line, keys_t, bias, sums, terms, term_out, term_in, dq_out, dq_in,
+    dq_ref, gko_ref, gvo_ref, gkn_ref, gvn_ref,
+    q_all, do_all, kv_all, line, grad_ref, keys_t, bias, sums, terms, term_out, term_in, dq_out, dq_in,
     q_send, q_recv, do_send, do_recv, kv_send, kv_recv, pass_send, dq_send, dq_recv, old_send, old_recv, new_send, new_recv,
 ):
     hb = heads_at_once
@@ -219,6 +219,11 @@
                 term_copy(group, 1, there, there).wait_recv()
                 grad_ref[group, 1] += term_in[group, 1, there].astype(jnp.float32)
 
+    for place, ref in enumerate((gko_ref, gvo_ref, gkn_ref, gvn_ref)):
+        left = place % 2 * width
+        for group in range(groups):
+            ref[:, group] = grad_ref[group, place // 2, :, left : left + width]
+
     kv_copy(partner, me_s).wait_send()
 
     @pl.loop(1, seqs // 2)
@@ -268,19 +273,20 @@
     seq_sems = pltpu.SemaphoreType.DMA((seqs,))
     term_sems = pltpu.SemaphoreType.DMA((groups, seqs))
     term_shape = (groups, 2, seqs, tokens, 2 * width)
-    dq, grads = pl.pallas_call(
+    dq, gko, gvo, gkn, gvn = pl.pallas_call(
         functools.partial(kernel, heads, seqs, per_group, hb),
         in_specs=[smem, smem] + [vmem] * 6,
-        out_specs=[vmem, vmem],
+        out_specs=[vmem] * 5,
         out_shape=[
             jax.ShapeDtypeStruct((all_heads, rows, width), narrow),
-            jax.ShapeDtypeStruct((groups, 2, tokens, 2 * width), wide),
-        ],
+        ]
+        + [jax.ShapeDtypeStruct(key_new.shape, wide)] * 4,
         scratch_shapes=[
             pltpu.VMEM(row_shape, narrow),
             pltpu.VMEM(row_shape, narrow),
             pltpu.VMEM((seqs, 4, tokens, groups * width), narrow),
             pltpu.VMEM((2, span, groups * width), narrow),
+            pltpu.VMEM((groups, 2, tokens, 2 * width), wide),
             pltpu.VMEM((width, span), narrow),
             pltpu.VMEM((span, tokens), wide),
             pltpu.VMEM((span, 2 * width), wide),
@@ -297,8 +303,7 @@
         ),
     )(windows, offset, by_head(query), by_head(grad_out), *kv)
     grad_query = lax.optimization_barrier(dq.transpose(1, 0, 2)).astype(wide)
-    grads = grads.reshape(groups, 2, tokens, 2, width).transpose(1, 3, 2, 0, 4)
-    return (grad_query, grads[1, 0], grads[1, 1], grads[0, 0], grads[0, 1])
+    return (grad_query, gkn, gvn, gko, gvo)
 
 
 def solution(mesh):

time: 76.9 us -> 78.5 us (1.021)
  local copies, waits for them, and re-layouts: 10.6 us -> 11.8 us
    unnamed x5 -> x15, local copies, waits for them, and re-layouts: 1.41 us -> 5.23 us
    reshape x2 -> x0, local copies, waits for them, and re-layouts: 1.78 us -> none  [shards(): grads = grads.reshape(groups, 2, tokens, 2, width).transpose(1, 3, 2, 0, 4)]
    squeeze x1 -> x0, local copies, waits for them, and re-layouts: 0.8 us -> none  [shards(): return (grad_query, grads[1, 0], grads[1, 1], grads[0, 0], grads[0, 1])]
where the time goes in v4:
time: 78.5 us; the launch traced here: 78.2 us
  Pallas kernels  65 us (83%)
  local copies, waits for them, and re-layouts  11.8 us (15%)
  between operations  1.41 us (2%)
    pallas_call x1, Pallas kernels, shards(): pl.pallas_call(functools.partial(kernel, heads, seqs, per_group, hb), in_...  65 us
    unnamed x15, local copies, waits for them, and re-layouts  5.23 us
    transpose x2, local copies, waits for them, and re-layouts, by_head(): return x.transpose(1, 0, 2).reshape(heads, mine, rows, width)  3.5 us
    reshape x2, local copies, waits for them, and re-layouts, shards(): x.reshape(tokens, groups * width)  3.07 us

profile of v4, /device:TPU:1, one launch (start us, length us, event | category | flops | bytes accessed | tf_op | source)
XLA Modules:
  0.0 78.2 jit_solution(17251888002110137499)
XLA Ops:
  0.6 0.0 copy-start
  1.4 1.5 %copy_bitcast_fusion = (bf16[128,256]{1,0:T(8,128)(2,1)}, bf16[128,256]{1,0:T(8,128)(2,1)}) fusion(bf16[16,8,2,128]{3,2,1,0:T(2,128)(2,1)} %bitcast.22, bf16[16,8,2,128]{3,2,1,0:T(2,128)(2,1)} %bitcast.23), kind=kLoop, calls=%fused_computation | loop fusion | bytes 262144 | tf_op jit(solution)/shard_map/reshape | solution.py:267
  2.9 1.5 %copy_bitcast_fusion.2 = (bf16[128,256]{1,0:T(8,128)(2,1)}, bf16[128,256]{1,0:T(8,128)(2,1)}) fusion(bf16[16,8,2,128]{3,2,1,0:T(2,128)(2,1)} %bitcast.24, bf16[16,8,2,128]{3,2,1,0:T(2,128)(2,1)} %bitcast.25), kind=kLoop, calls=%fused_computation.2 | loop fusion | bytes 262144 | tf_op jit(solution)/shard_map/reshape | solution.py:267
  4.4 2.3 %copy.13 = bf16[96,32,128]{2,1,0:T(8,128)(2,1)} copy(bf16[96,32,128]{2,0,1:T(8,128)(2,1)} %bitcast.19) | data formatting | bytes 1572864 | tf_op jit(solution)/shard_map/transpose | solution.py:265
  6.8 0.0 copy-done
  6.8 1.2 %copy.14 = bf16[96,32,128]{2,1,0:T(8,128)(2,1)} copy(bf16[96,32,128]{2,0,1:T(8,128)(2,1)S(1)} %bitcast.20) | data formatting | bytes 1572864 | tf_op jit(solution)/shard_map/transpose | solution.py:265
  7.9 65.0 %shard_map.119 = (bf16[96,32,128]{2,1,0:T(8,128)(2,1)}, f32[128,2,128]{2,1,0:T(2,128)}, f32[128,2,128]{2,1,0:T(2,128)}, f32[128,2,128]{2,1,0:T(2,128)}, f32[128,2,128]{2,1,0:T(2,128)}) custom-call(s32[2]{0:T(128)} %win_ref.1, s32[1]{0:T(128)S(6)} %copy.28.off_ref, bf16[4,24,32,128]{3,2,1,0:T(8,128)(2,1)} %bitcast.17, bf16[4,24,32,128]{3,2,1,0:T(8,128)(2,1)} %bitcast.18, ...), custom_call_target="tpu_custom_call" | custom-call | tf_op jit(solution)/shard_map/pallas_call | solution.py:276
  72.9 0.0 copy-start.4
  72.9 0.0 copy-start.3
  72.9 0.0 copy-start.2
  72.9 0.0 copy-start.1
  73.0 2.6 %copy.15 = f32[32,96,128]{2,1,0:T(8,128)} copy(bf16[32,96,128]{2,0,1:T(8,128)(2,1)} %bitcast.21) | data formatting | bytes 2359296
  75.5 0.0 copy-done.4
  75.5 0.7 copy.29
  76.2 0.0 copy-done.3
  76.2 0.7 copy.30
  76.9 0.0 copy-done.2
  76.9 0.7 copy.31
  77.5 0.0 copy-done.1
  77.5 0.7 copy.32
Async XLA Ops:
  0.6 6.1 %copy-start = (bf16[32,96,128]{2,1,0:T(8,128)(2,1)S(1)}, bf16[32,96,128]{2,1,0:T(8,128)(2,1)}, u32[]{:S(2)}) copy-start(bf16[32,96,128]{2,1,0:T(8,128)(2,1)} %param.15) | copy-start | bytes 2359300
  72.9 2.6 %copy-start.4 = (f32[128,2,128]{2,1,0:T(2,128)S(1)}, f32[128,2,128]{2,1,0:T(2,128)}, u32[]{:S(2)}) copy-start(f32[128,2,128]{2,1,0:T(2,128)} %get-tuple-element.30) | copy-start | bytes 393220
  72.9 3.3 %copy-start.3 = (f32[128,2,128]{2,1,0:T(2,128)S(1)}, f32[128,2,128]{2,1,0:T(2,128)}, u32[]{:S(2)}) copy-start(f32[128,2,128]{2,1,0:T(2,128)} %get-tuple-element.31) | copy-start | bytes 393220
  72.9 3.9 %copy-start.2 = (f32[128,2,128]{2,1,0:T(2,128)S(1)}, f32[128,2,128]{2,1,0:T(2,128)}, u32[]{:S(2)}) copy-start(f32[128,2,128]{2,1,0:T(2,128)} %get-tuple-element.32) | copy-start | bytes 393220
  72.9 4.6 %copy-start.1 = (f32[128,2,128]{2,1,0:T(2,128)S(1)}, f32[128,2,128]{2,1,0:T(2,128)}, u32[]{:S(2)}) copy-start(f32[128,2,128]{2,1,0:T(2,128)} %get-tuple-element.33) | copy-start | bytes 393220
